TPU v7x, 256 devices: a whole 4x4x8 slice. The times are simulated.
256 devices in a mesh: pipe: 8 (over z), expert: 32 (over x, y, core).
Axes of the slice: x: 4, y: 4, z: 8, core: 2. Of those that a mesh axis runs over, the one named last changes fastest.
Arguments:
- inputs: bfloat16 [8, 4096, 4096], P('pipe', 'expert'), may hold values from -6 to 6
- upstream: bfloat16 [8, 4096, 4096], P('pipe', 'expert'), may hold values from -24 to 24
- route: int32 [8, 4096, 8], P('pipe', 'expert'), may hold values from 0 to 127, as said below
- prob: float32 [8, 4096, 8], P('pipe', 'expert'), may hold values from 0.05 to 0.4
- gate_up: bfloat16 [8, 32, 4096, 384], P('pipe', 'expert'), may hold values from -0.09375 to 0.09375
- down: bfloat16 [8, 32, 192, 4096], P('pipe', 'expert'), may hold values from -0.15625 to 0.15625
Outputs:
- grad_input: bfloat16 [8, 4096, 4096], P('pipe', 'expert')
- grad_gate_up: bfloat16 [8, 32, 4096, 384], P('pipe', 'expert')
- grad_down: bfloat16 [8, 32, 192, 4096], P('pipe', 'expert')
Inputs may be any that keep to these rules, and one draw needn't show every extreme that they name: `route`: each token names 8 different experts and at most one expert below 4. In each aligned block of 128 tokens of a section every expert below 4 is named by 1 to 8 tokens; one such expert, the same for all blocks, is named by exactly 8 tokens of every block.
All inputs are finite; a program needn't handle non-finite values.
Results may differ from a plain program's by a relative error of at most 0.014.
Values may be sent and summed in bfloat16 or wider, within the bound.
No kernel may reach another device: no remote copies, remote signals or barrier semaphores. Data moves between devices by JAX's collectives and lax.ppermute only.
A program may use at most 128 MiB of HBM per device.

v0:
```python
import jax
import jax.numpy as jnp
from jax import lax
from jax.sharding import PartitionSpec as P

SPLIT = 8
CAP = 8


def shifted(block, axis, distance):
    devices = range(lax.axis_size(axis))
    route = [((i - distance) % len(devices), i) for i in devices]
    return lax.ppermute(block, axis, route)


def shards(inputs, upstream, route, prob, gate_up, down):
    arrived = shifted(upstream, "pipe", -1)[0]
    layer_in = inputs[0]
    slot_route = route[0]
    slot_prob = prob[0]
    groups = lax.axis_size("expert")
    flight = groups // SPLIT
    width = layer_in.shape[1]
    experts_here = jnp.arange(flight, dtype=jnp.int32)
    hits = slot_route[:, :, None] == experts_here[None, None, :]
    weight = jnp.sum(jnp.where(hits, slot_prob[:, :, None], jnp.float32(0.0)), axis=1)
    member = jnp.any(hits, axis=1).astype(jnp.int32)
    rank = jnp.cumsum(member, axis=0) - member
    slot_ids = jnp.arange(CAP, dtype=jnp.int32)
    select = (member.T[:, None, :] == 1) & (rank.T[:, None, :] == slot_ids[None, :, None])
    picker = select.astype(jnp.bfloat16)
    rows_x = jnp.einsum("ect,td->ecd", picker, layer_in, preferred_element_type=jnp.float32).astype(
        jnp.bfloat16
    )
    rows_g = jnp.einsum("ect,td->ecd", picker, arrived, preferred_element_type=jnp.float32)
    slot_weight = jnp.sum(jnp.where(select, weight.T[:, None, :], jnp.float32(0.0)), axis=2)
    rows_e = (rows_g * slot_weight[:, :, None]).astype(jnp.bfloat16)
    mine = lax.axis_index("expert") // SPLIT
    all_x, all_e = (
        lax.all_gather(rows_x[None], "expert", axis=0, tiled=True),
        lax.all_gather(rows_e[None], "expert", axis=0, tiled=True),
    )
    got_x = lax.dynamic_index_in_dim(all_x, mine, axis=1, keepdims=False)
    got_e = lax.dynamic_index_in_dim(all_e, mine, axis=1, keepdims=False)
    flat_x = got_x.reshape(-1, width)
    flat_e = got_e.reshape(-1, width)
    w_both = gate_up[0, 0]
    w_down = down[0, 0]
    hidden_cols = w_down.shape[0]
    both = jnp.dot(flat_x, w_both, preferred_element_type=jnp.float32)
    pre_gate = both[:, :hidden_cols]
    pre_up = both[:, hidden_cols:]
    sigma = jax.nn.sigmoid(pre_gate)
    silu_val = pre_gate * sigma
    hidden = (silu_val * pre_up).astype(jnp.bfloat16)
    grad_hidden = lax.dot_general(
        flat_e, w_down, (((1,), (1,)), ((), ())), preferred_element_type=jnp.float32
    )
    grad_a = (grad_hidden * pre_up * sigma * (1.0 + pre_gate * (1.0 - sigma))).astype(jnp.bfloat16)
    grad_u = (grad_hidden * silu_val).astype(jnp.bfloat16)
    grad_both = jnp.concatenate([grad_a, grad_u], axis=1)
    grad_down = lax.dot_general(
        hidden, flat_e, (((0,), (0,)), ((), ())), preferred_element_type=jnp.float32
    ).astype(jnp.bfloat16)
    grad_gu = lax.dot_general(
        flat_x, grad_both, (((0,), (0,)), ((), ())), preferred_element_type=jnp.float32
    ).astype(jnp.bfloat16)
    partial_value = lax.dot_general(
        grad_both, w_both, (((1,), (1,)), ((), ())), preferred_element_type=jnp.float32
    ).astype(jnp.bfloat16)
    returned = lax.all_to_all(
        partial_value.reshape(groups, CAP, width), "expert", split_axis=0, concat_axis=0, tiled=True
    )
    summed = jnp.sum(returned.astype(jnp.float32).reshape(flight, SPLIT, CAP, width), axis=1)
    grad_x = jnp.einsum(
        "ect,ecd->td", select.astype(jnp.float32), summed, precision=lax.Precision.HIGHEST
    )
    return (grad_x.astype(jnp.bfloat16)[None], grad_gu[None, None], grad_down[None, None])


def solution(mesh):
    placed = (
        P("pipe", "expert", None),
        P("pipe", "expert", None),
        P("pipe", "expert", None),
        P("pipe", "expert", None),
        P("pipe", "expert", None, None),
        P("pipe", "expert", None, None),
    )
    return jax.shard_map(
        shards,
        mesh=mesh,
        in_specs=placed,
        out_specs=(
            P("pipe", "expert", None),
            P("pipe", "expert", None, None),
            P("pipe", "expert", None, None),
        ),
        check_vma=False,
    )
```

profile of v0, /device:TPU:1, one launch (start us, length us, event | category | flops | bytes accessed | tf_op | source)
XLA Modules:
  0.0 184.6 jit_solution(6764796481486024812)
XLA Ops:
  7.2 0.0 copy-start
  7.2 0.0 all-gather.7.cloned.1.call-start
  7.2 0.9 fusion.23
  8.1 0.1 copy.29
  8.2 0.2 reduce_window_sum.11
  8.4 0.1 copy.30
  8.4 2.2 %convolution_convert_fusion.3 = bf16[4,8,4096]{2,1,0:T(8,128)(2,1)} fusion(bf16[1,128,4096]{2,1,0:T(8,128)(2,1)} %param.6, s32[4,128]{1,0:T(4,128)S(1)} %subtract_bitcast_fusion, pred[4,128]{1,0:T(4,128)(4,1)S(1)} %get-tuple-element.5), kind=kOutput, calls=%fused_computation.11 | convolution fusion | flops 33693696 | bytes 1313280 | tf_op jit(solution)/shard_map/ect,td->ecd/dot_general | solution.py:32
  10.7 0.0 all-gather.7.cloned.1.call-update
  10.7 0.0 all-gather.5.cloned.1.call-start
  10.7 6.5 %collective-permute-start = (bf16[1,128,4096]{2,1,0:T(8,128)(2,1)}, bf16[1,128,4096]{2,1,0:T(8,128)(2,1)S(1)}, u32[]{:S(2)}, u32[]{:S(2)}) collective-permute-start(bf16[1,128,4096]{2,1,0:T(8,128)(2,1)} %param.7), channel_id=1, source_target_pairs={{32,0},{64,32},{96,64},{128,96},{160,128},{192,160},{224,192},{0,2... | collective-permute-start | bytes 3145736 | tf_op jit(solution)/shard_map/ppermute | solution.py:13
  17.2 0.7 select_reduce_fusion.1
  17.9 0.1 select_reduce_fusion
  18.0 21.3 %collective-permute-done = bf16[1,128,4096]{2,1,0:T(8,128)(2,1)S(1)} collective-permute-done((bf16[1,128,4096]{2,1,0:T(8,128)(2,1)}, bf16[1,128,4096]{2,1,0:T(8,128)(2,1)S(1)}, u32[]{:S(2)}, u32[]{:S(2)}) %collective-permute-start) | collective-permute-done | bytes 1048608 | tf_op jit(solution)/shard_map/ppermute | solution.py:13
  39.4 1.0 fusion.5
  40.3 0.0 all-gather.5.cloned.1.call-update
  40.4 32.8 %all-gather.7.cloned.1.call-done = bf16[128,8,4096]{2,1,0:T(8,128)(2,1)} async-done(((bf16[4,8,4096]{2,1,0:T(8,128)(2,1)}), bf16[128,8,4096]{2,1,0:T(8,128)(2,1)}) %all-gather.7.cloned.1.call-update) | async-done | bytes 8388624 | tf_op jit(solution)/shard_map/all_gather | solution.py:40
  73.1 0.0 copy-done
  73.1 2.9 %fusion.7 = f32[256,384]{0,1:T(8,128)S(1)} fusion(bf16[1,1,4096,384]{3,2,1,0:T(8,128)(2,1)S(1)} %copy-done, bf16[32,4,8,4096]{3,2,1,0:T(8,128)(2,1)} %bitcast.63, s32[]{:T(128)S(6)} %select_n.21), kind=kOutput, calls=%fused_computation.14 | convolution fusion | flops 805306368 | bytes 5636100 | tf_op jit(solution)/shard_map/dot_general | solution.py:50
  76.1 57.7 %all-gather.5.cloned.1.call-done = bf16[128,8,4096]{2,1,0:T(8,128)(2,1)} async-done(((bf16[4,8,4096]{2,1,0:T(8,128)(2,1)}), bf16[128,8,4096]{2,1,0:T(8,128)(2,1)}) %all-gather.5.cloned.1.call-update) | async-done | bytes 8388624 | tf_op jit(solution)/shard_map/all_gather | solution.py:41
  133.7 2.9 %multiply_convert_fusion.2 = (bf16[256,192]{0,1:T(8,128)(2,1)S(1)}, bf16[256,192]{0,1:T(8,128)(2,1)S(1)}) fusion(f32[256,384]{0,1:T(8,128)S(1)} %fusion.7, bf16[1,1,192,4096]{3,2,1,0:T(8,128)(2,1)} %param.11, bf16[32,4,8,4096]{3,2,1,0:T(8,128)(2,1)} %bitcast.57, s32[]{:T(128)S(6)} %select_n.21), kind=kOutput, calls=%fused_computation.31 | convolution fusion | flops 403292160 | bytes 4259844 | tf_op jit(solution)/shard_map/dot_general | solution.py:56
  136.6 0.0 copy-start.1
  136.6 0.0 copy-start.2
  136.7 0.6 copy-done.1
  137.3 0.0 copy-done.2
  137.3 2.6 %fusion.1 = bf16[32,8,4096]{2,1,0:T(8,128)(2,1)} fusion(bf16[1,1,4096,384]{3,2,1,0:T(8,128)(2,1)S(1)} %copy-done, bf16[256,192]{0,1:T(8,128)(2,1)S(1)} %get-tuple-element.4, bf16[256,192]{0,1:T(8,128)(2,1)S(1)} %get-tuple-element.3), kind=kOutput, calls=%fused_computation.4 | convolution fusion | flops 806748160 | bytes 5439488 | tf_op jit(solution)/shard_map/dot_general | solution.py:68
  139.9 5.5 %all-to-all-start = ((bf16[32,8,4096]{2,1,0:T(8,128)(2,1)}), bf16[32,8,4096]{2,1,0:T(8,128)(2,1)}, u32[]{:S(2)}, u32[]{:S(2)}) async-start(bf16[32,8,4096]{2,1,0:T(8,128)(2,1)} %fusion.1), calls=%async_computation | async-start | bytes 4194304 | tf_op jit(solution)/shard_map/all_to_all | solution.py:71
  145.4 4.6 %fusion = bf16[1,1,4096,384]{3,2,1,0:T(8,128)(2,1)} fusion(bf16[32,4,8,4096]{3,2,1,0:T(8,128)(2,1)} %bitcast.64, s32[]{:T(128)S(6)} %select_n.21, bf16[256,192]{0,1:T(8,128)(2,1)} %copy-done.2, bf16[256,192]{0,1:T(8,128)(2,1)} %copy-done.1), kind=kOutput, calls=%fused_computation.2 | convolution fusion | flops 807272448 | bytes 5439492 | tf_op jit(solution)/shard_map/dot_general | solution.py:65
  150.0 3.3 %fusion.3 = bf16[1,1,192,4096]{3,2,1,0:T(8,128)(2,1)} fusion(bf16[32,4,8,4096]{3,2,1,0:T(8,128)(2,1)} %bitcast.58, s32[]{:T(128)S(6)} %select_n.21, f32[256,384]{0,1:T(8,128)S(1)} %fusion.7), kind=kOutput, calls=%fused_computation.7 | convolution fusion | flops 403734528 | bytes 4063236 | tf_op jit(solution)/shard_map/dot_general | solution.py:62
  153.3 20.5 %all-to-all-done = bf16[32,8,4096]{2,1,0:T(8,128)(2,1)} async-done(((bf16[32,8,4096]{2,1,0:T(8,128)(2,1)}), bf16[32,8,4096]{2,1,0:T(8,128)(2,1)}, u32[]{:S(2)}, u32[]{:S(2)}) %all-to-all-start) | async-done | bytes 2097184 | tf_op jit(solution)/shard_map/all_to_all | solution.py:71
  173.8 2.0 %convert_reduce_fusion = f32[4,8,4096]{2,1,0:T(8,128)S(1)} fusion(bf16[32,8,4096]{2,1,0:T(8,128)(2,1)} %all-to-all-done), kind=kLoop, calls=%fused_computation.12 | loop fusion | flops 1966080 | bytes 2621440 | tf_op jit(solution)/shard_map/reduce_sum | solution.py:74
  175.8 2.0 %fusion.4 = bf16[1,128,4096]{2,1,0:T(8,128)(2,1)} fusion(f32[4,8,4096]{2,1,0:T(8,128)S(1)} %convert_reduce_fusion, s32[4,128]{1,0:T(4,128)S(1)} %subtract_bitcast_fusion, pred[4,128]{1,0:T(4,128)(4,1)S(1)} %get-tuple-element.5), kind=kOutput, calls=%fused_computation.8 | convolution fusion | flops 201859072 | bytes 1575424 | tf_op jit(solution)/shard_map/ect,ecd->td/dot_general | solution.py:75
  (2 shorter events, 0.0 us)
Async XLA Ops:
  7.2 66.0 %copy-start = (bf16[1,1,4096,384]{3,2,1,0:T(8,128)(2,1)S(1)}, bf16[1,1,4096,384]{3,2,1,0:T(8,128)(2,1)}, u32[]{:S(2)}) copy-start(bf16[1,1,4096,384]{3,2,1,0:T(8,128)(2,1)} %param.10) | copy-start | bytes 9437188
  7.2 66.0 %all-gather.7.cloned.1.call-start = ((), (), s32[]{:S(2)}) async-start(), calls=%async_computation.2 | async-start | bytes 8650752 | tf_op jit(solution)/shard_map/all_gather | solution.py:40
  10.7 123.0 %all-gather.5.cloned.1.call-start = ((), (), s32[]{:S(2)}) async-start(), calls=%async_computation.1 | async-start | bytes 8650752 | tf_op jit(solution)/shard_map/all_gather | solution.py:41
  10.7 28.6 %collective-permute-start = (bf16[1,128,4096]{2,1,0:T(8,128)(2,1)}, bf16[1,128,4096]{2,1,0:T(8,128)(2,1)S(1)}, u32[]{:S(2)}, u32[]{:S(2)}) collective-permute-start(bf16[1,128,4096]{2,1,0:T(8,128)(2,1)} %param.7), channel_id=1, source_target_pairs={{32,0},{64,32},{96,64},{128,96},{160,128},{192,160},{224,192},{0,2... | collective-permute-start | bytes 3145736 | tf_op jit(solution)/shard_map/ppermute | solution.py:13
  136.6 0.6 copy-start.1
  136.6 0.7 copy-start.2
  139.9 33.9 %all-to-all-start = ((bf16[32,8,4096]{2,1,0:T(8,128)(2,1)}), bf16[32,8,4096]{2,1,0:T(8,128)(2,1)}, u32[]{:S(2)}, u32[]{:S(2)}) async-start(bf16[32,8,4096]{2,1,0:T(8,128)(2,1)} %fusion.1), calls=%async_computation | async-start | bytes 4194304 | tf_op jit(solution)/shard_map/all_to_all | solution.py:71
Sparse Core Ops, SparseCore 0:
  11.1 61.9 all-gather.6
  76.3 57.4 all-gather.4
where the time goes:
time: 185 us
  waiting for transfers between devices  132 us (71%)
  matrix products  21.5 us (12%)
  between operations  14.1 us (8%)
  starting transfers between devices  12.1 us (7%)
  other arithmetic  3.82 us (2%)
    all_gather x1, waiting for transfers between devices, shards(): lax.all_gather(rows_e[None], 'expert', axis=0, tiled=True)  57.7 us
    all_gather x1, waiting for transfers between devices, shards(): lax.all_gather(rows_x[None], 'expert', axis=0, tiled=True)  32.8 us
    ppermute x1, waiting for transfers between devices, shifted(): return lax.ppermute(block, axis, route)  21.3 us
    all_to_all x1, waiting for transfers between devices, shards(): lax.all_to_all(partial_value.reshape(groups, CAP, width), 'expert', split...  20.5 us
    ppermute x1, starting transfers between devices, shifted(): return lax.ppermute(block, axis, route)  6.47 us
    all_to_all x1, starting transfers between devices, shards(): lax.all_to_all(partial_value.reshape(groups, CAP, width), 'expert', split...  5.54 us
    dot_general x1, matrix products, shards(): lax.dot_general(flat_x, grad_both, (((0,), (0,)), ((), ())), preferred_el...  4.57 us
  transfers between devices with their start and end apart: 4, of which 4 were waited for; matrix products, arithmetic and copies ran while one was open for 7% of the time, Pallas kernels for 0%

commit v1 on v0

--- a/solution.py
+++ b/solution.py
@@ -37,7 +37,10 @@
     rows_e = (rows_g * slot_weight[:, :, None]).astype(jnp.bfloat16)
     mine = lax.axis_index("expert") // SPLIT
     all_x, all_e = (
-        lax.all_gather(rows_x[None], "expert", axis=0, tiled=True),
+        jnp.concatenate(
+            lax.all_to_all(jnp.stack([rows_x[None]] * lax.axis_size("expert")), "expert", 0, 0),
+            axis=0,
+        ),
         lax.all_gather(rows_e[None], "expert", axis=0, tiled=True),
     )
     got_x = lax.dynamic_index_in_dim(all_x, mine, axis=1, keepdims=False)

time: 185 us -> 246 us (1.33)
  waiting for transfers between devices: 132 us -> 164 us
  starting transfers between devices: 12.1 us -> 36.7 us
  local copies, waits for them, and re-layouts: 0.84 us -> 5.11 us
    all_to_all x0 -> x1, waiting for transfers between devices: none -> 123 us  [shards(): lax.all_to_all(jnp.stack([rows_x[None]] * lax.axis_size('expert')), 'expe...]
    all_gather x1, waiting for transfers between devices: 57.7 us -> 0.02 us  [shards(): lax.all_gather(rows_e[None], 'expert', axis=0, tiled=True)]
    all_gather x1 -> x0, waiting for transfers between devices: 32.8 us -> none  [shards(): lax.all_gather(rows_x[None], 'expert', axis=0, tiled=True)]
    all_to_all x1, starting transfers between devices: 5.54 us -> 21.6 us  [shards(): lax.all_to_all(partial_value.reshape(groups, CAP, width), 'expert', split...]
    all_to_all x0 -> x1, starting transfers between devices: none -> 8.67 us  [shards(): lax.all_to_all(jnp.stack([rows_x[None]] * lax.axis_size('expert')), 'expe...]
    another operation x0 -> x1, local copies, waits for them, and re-layouts: none -> 4.27 us  [shards(): jnp.stack([rows_x[None]] * lax.axis_size('expert'))]
  transfers between devices with their start and end apart: 4 -> 4, of which waited for: 4 -> 3; matrix products, arithmetic and copies ran while one was open for 7% -> 8% of each run, Pallas kernels for 0% -> 0%
where the time goes in v1:
time: 246 us; the launch traced here: 245 us
  waiting for transfers between devices  164 us (67%)
  starting transfers between devices  36.7 us (15%)
  matrix products  22 us (9%)
  between operations  14.1 us (6%)
  local copies, waits for them, and re-layouts  5.11 us (2%)
  other arithmetic  3.68 us (1%)
    all_to_all x1, waiting for transfers between devices, shards(): lax.all_to_all(jnp.stack([rows_x[None]] * lax.axis_size('expert')), 'expe...  123 us
    all_to_all x1, starting transfers between devices, shards(): lax.all_to_all(partial_value.reshape(groups, CAP, width), 'expert', split...  21.6 us
    all_to_all x1, waiting for transfers between devices, shards(): lax.all_to_all(partial_value.reshape(groups, CAP, width), 'expert', split...  20.5 us
    ppermute x1, waiting for transfers between devices, shifted(): return lax.ppermute(block, axis, route)  20.3 us
    all_to_all x1, starting transfers between devices, shards(): lax.all_to_all(jnp.stack([rows_x[None]] * lax.axis_size('expert')), 'expe...  8.67 us
    ppermute x1, starting transfers between devices, shifted(): return lax.ppermute(block, axis, route)  6.47 us
  transfers between devices with their start and end apart: 4, of which 3 were waited for; matrix products, arithmetic and copies ran while one was open for 8% of the time, Pallas kernels for 0%

profile of v1, /device:TPU:1, one launch (start us, length us, event | category | flops | bytes accessed | tf_op | source)
XLA Modules:
  0.0 245.4 jit_solution(2204515973264651644)
XLA Ops:
  7.2 0.0 copy-start
  7.2 0.0 all-gather.3.cloned.1.call-start
  7.2 6.5 %collective-permute-start = (bf16[1,128,4096]{2,1,0:T(8,128)(2,1)}, bf16[1,128,4096]{2,1,0:T(8,128)(2,1)}, u32[]{:S(2)}, u32[]{:S(2)}) collective-permute-start(bf16[1,128,4096]{2,1,0:T(8,128)(2,1)} %param.7), channel_id=1, source_target_pairs={{32,0},{64,32},{96,64},{128,96},{160,128},{192,160},{224,192},{0,2... | collective-permute-start | bytes 3145736 | tf_op jit(solution)/shard_map/ppermute | solution.py:13
  13.7 0.7 fusion.23
  14.4 0.1 copy.29
  14.5 0.2 reduce_window_sum.11
  14.7 0.1 copy.30
  14.8 0.7 select_reduce_fusion.1
  15.5 0.1 select_reduce_fusion
  15.6 20.3 %collective-permute-done = bf16[1,128,4096]{2,1,0:T(8,128)(2,1)} collective-permute-done((bf16[1,128,4096]{2,1,0:T(8,128)(2,1)}, bf16[1,128,4096]{2,1,0:T(8,128)(2,1)}, u32[]{:S(2)}, u32[]{:S(2)}) %collective-permute-start) | collective-permute-done | bytes 1048608 | tf_op jit(solution)/shard_map/ppermute | solution.py:13
  35.9 2.2 fusion.5
  38.1 0.0 all-gather.3.cloned.1.call-update
  38.1 1.5 convolution_convert_fusion.3
  39.6 4.3 %stack.3 = bf16[32,1,4,8,4096]{4,3,2,1,0:T(8,128)(2,1)} broadcast(bf16[4,8,4096]{2,1,0:T(8,128)(2,1)S(1)} %convolution_convert_fusion.3), dimensions={2,3,4} | broadcast | bytes 8650752 | tf_op jit(solution)/shard_map/stack | solution.py:41
  43.8 8.7 %all-to-all-start = ((bf16[32,1,4,8,4096]{4,3,2,1,0:T(8,128)(2,1)}), bf16[32,1,4,8,4096]{4,3,2,1,0:T(8,128)(2,1)}, u32[]{:S(2)}, u32[]{:S(2)}) async-start(bf16[32,1,4,8,4096]{4,3,2,1,0:T(8,128)(2,1)} %stack.3), calls=%async_computation | async-start | bytes 16777216 | tf_op jit(solution)/shard_map/all_to_all | solution.py:41
  52.5 123.0 %all-to-all-done = bf16[32,1,4,8,4096]{4,3,2,1,0:T(8,128)(2,1)} async-done(((bf16[32,1,4,8,4096]{4,3,2,1,0:T(8,128)(2,1)}), bf16[32,1,4,8,4096]{4,3,2,1,0:T(8,128)(2,1)}, u32[]{:S(2)}, u32[]{:S(2)}) %all-to-all-start) | async-done | bytes 8388640 | tf_op jit(solution)/shard_map/all_to_all | solution.py:41
  175.5 0.0 copy-done
  175.5 2.9 %fusion.7 = f32[256,384]{0,1:T(8,128)S(1)} fusion(bf16[1,1,4096,384]{3,2,1,0:T(8,128)(2,1)S(1)} %copy-done, bf16[32,1,4,8,4096]{4,3,2,1,0:T(8,128)(2,1)} %all-to-all-done, s32[]{:T(128)S(6)} %select_n.21), kind=kOutput, calls=%fused_computation.14 | convolution fusion | flops 805306368 | bytes 5636100 | tf_op jit(solution)/shard_map/dot_general | solution.py:53
  178.5 0.0 all-gather.3.cloned.1.call-done
  178.5 2.9 %multiply_convert_fusion.2 = (bf16[256,192]{0,1:T(8,128)(2,1)S(1)}, bf16[256,192]{0,1:T(8,128)(2,1)S(1)}) fusion(f32[256,384]{0,1:T(8,128)S(1)} %fusion.7, bf16[1,1,192,4096]{3,2,1,0:T(8,128)(2,1)} %param.11, bf16[32,4,8,4096]{3,2,1,0:T(8,128)(2,1)} %bitcast.56, s32[]{:T(128)S(6)} %select_n.21), kind=kOutput, calls=%fused_computation.31 | convolution fusion | flops 403292160 | bytes 4259844 | tf_op jit(solution)/shard_map/dot_general | solution.py:59
  181.4 0.0 copy-start.1
  181.4 0.0 copy-start.2
  181.4 0.6 copy-done.1
  182.0 0.0 copy-done.2
  182.1 2.6 %fusion.1 = bf16[32,8,4096]{2,1,0:T(8,128)(2,1)} fusion(bf16[1,1,4096,384]{3,2,1,0:T(8,128)(2,1)S(1)} %copy-done, bf16[256,192]{0,1:T(8,128)(2,1)S(1)} %get-tuple-element.4, bf16[256,192]{0,1:T(8,128)(2,1)S(1)} %get-tuple-element.3), kind=kOutput, calls=%fused_computation.4 | convolution fusion | flops 806748160 | bytes 5439488 | tf_op jit(solution)/shard_map/dot_general | solution.py:71
  184.7 21.6 %all-to-all-start.1 = ((bf16[32,8,4096]{2,1,0:T(8,128)(2,1)}), bf16[32,8,4096]{2,1,0:T(8,128)(2,1)}, u32[]{:S(2)}, u32[]{:S(2)}) async-start(bf16[32,8,4096]{2,1,0:T(8,128)(2,1)} %fusion.1), calls=%async_computation.1 | async-start | bytes 4194304 | tf_op jit(solution)/shard_map/all_to_all | solution.py:74
  206.2 4.6 %fusion = bf16[1,1,4096,384]{3,2,1,0:T(8,128)(2,1)} fusion(bf16[32,1,4,8,4096]{4,3,2,1,0:T(8,128)(2,1)} %all-to-all-done, s32[]{:T(128)S(6)} %select_n.21, bf16[256,192]{0,1:T(8,128)(2,1)} %copy-done.2, bf16[256,192]{0,1:T(8,128)(2,1)} %copy-done.1), kind=kOutput, calls=%fused_computation.2 | convolution fusion | flops 807272448 | bytes 5439492 | tf_op jit(solution)/shard_map/dot_general | solution.py:68
  210.8 3.3 %fusion.3 = bf16[1,1,192,4096]{3,2,1,0:T(8,128)(2,1)} fusion(bf16[32,4,8,4096]{3,2,1,0:T(8,128)(2,1)} %bitcast.57, s32[]{:T(128)S(6)} %select_n.21, f32[256,384]{0,1:T(8,128)S(1)} %fusion.7), kind=kOutput, calls=%fused_computation.7 | convolution fusion | flops 403734528 | bytes 4063236 | tf_op jit(solution)/shard_map/dot_general | solution.py:65
  214.1 20.5 %all-to-all-done.1 = bf16[32,8,4096]{2,1,0:T(8,128)(2,1)} async-done(((bf16[32,8,4096]{2,1,0:T(8,128)(2,1)}), bf16[32,8,4096]{2,1,0:T(8,128)(2,1)}, u32[]{:S(2)}, u32[]{:S(2)}) %all-to-all-start.1) | async-done | bytes 2097184 | tf_op jit(solution)/shard_map/all_to_all | solution.py:74
  234.6 2.0 convert_reduce_fusion
  236.6 2.0 fusion.4
  (2 shorter events, 0.0 us)
Async XLA Ops:
  7.2 168.4 %copy-start = (bf16[1,1,4096,384]{3,2,1,0:T(8,128)(2,1)S(1)}, bf16[1,1,4096,384]{3,2,1,0:T(8,128)(2,1)}, u32[]{:S(2)}) copy-start(bf16[1,1,4096,384]{3,2,1,0:T(8,128)(2,1)} %param.10) | copy-start | bytes 9437188
  7.2 171.3 %all-gather.3.cloned.1.call-start = ((), (), s32[]{:S(2)}) async-start(), calls=%async_computation.2 | async-start | bytes 8650752 | tf_op jit(solution)/shard_map/all_gather | solution.py:44
  7.2 28.6 %collective-permute-start = (bf16[1,128,4096]{2,1,0:T(8,128)(2,1)}, bf16[1,128,4096]{2,1,0:T(8,128)(2,1)}, u32[]{:S(2)}, u32[]{:S(2)}) collective-permute-start(bf16[1,128,4096]{2,1,0:T(8,128)(2,1)} %param.7), channel_id=1, source_target_pairs={{32,0},{64,32},{96,64},{128,96},{160,128},{192,160},{224,192},{0,2... | collective-permute-start | bytes 3145736 | tf_op jit(solution)/shard_map/ppermute | solution.py:13
  43.8 131.7 %all-to-all-start = ((bf16[32,1,4,8,4096]{4,3,2,1,0:T(8,128)(2,1)}), bf16[32,1,4,8,4096]{4,3,2,1,0:T(8,128)(2,1)}, u32[]{:S(2)}, u32[]{:S(2)}) async-start(bf16[32,1,4,8,4096]{4,3,2,1,0:T(8,128)(2,1)} %stack.3), calls=%async_computation | async-start | bytes 16777216 | tf_op jit(solution)/shard_map/all_to_all | solution.py:41
  181.4 0.6 copy-start.1
  181.4 0.7 copy-start.2
  184.7 50.0 %all-to-all-start.1 = ((bf16[32,8,4096]{2,1,0:T(8,128)(2,1)}), bf16[32,8,4096]{2,1,0:T(8,128)(2,1)}, u32[]{:S(2)}, u32[]{:S(2)}) async-start(bf16[32,8,4096]{2,1,0:T(8,128)(2,1)} %fusion.1), calls=%async_computation.1 | async-start | bytes 4194304 | tf_op jit(solution)/shard_map/all_to_all | solution.py:74
Sparse Core Ops, SparseCore 0:
  38.2 132.9 all-gather.2
